TPU v7x, 256 devices: a whole 4x4x8 slice. The times are simulated.
256 devices in a mesh: row: 32 (over x, y, core), col: 8 (over z).
Axes of the slice: x: 4, y: 4, z: 8, core: 2. Of those that a mesh axis runs over, the one named last changes fastest.
Arguments:
- matrix: float32 [65536, 5, 8, 128], P('row', None, 'col'), may hold values from -320 to 320, as said below
Outputs:
- r_rows: float32 [256, 5, 8, 128], P(None, None, 'col')
- residual: float32 [65536, 5, 8, 128], P('row', None, 'col')
Inputs may be any that keep to these rules, and one draw needn't show every extreme that they name: `matrix`: real entries; the first 256 columns have full column rank on every block of 2048 rows.
All inputs are finite; a program needn't handle non-finite values.
Results may differ from a plain program's by a relative error of at most 0.0003.
Values sent between devices are 32-bit elements; how exact they have to be, the bound alone decides.
No kernel may reach another device: no remote copies, remote signals or barrier semaphores. Data moves between devices by JAX's collectives and lax.ppermute only.
A program may use at most 128 MiB of HBM per device.

v0:
```python
import math
import jax
import jax.numpy as jnp
from jax import lax
from jax.sharding import PartitionSpec as P


def broadcast(value, axis, root):
    mine = lax.axis_index(axis) == root
    return lax.psum(jnp.where(mine, value, jnp.zeros_like(value)), axis)


def cross_product(left, right):
    return jnp.einsum(
        "mk,mn->kn",
        left,
        right,
        precision=lax.Precision.HIGHEST,
        preferred_element_type=jnp.float32,
    )


def matmul(left, right):
    return jnp.dot(left, right, precision=lax.Precision.HIGHEST, preferred_element_type=jnp.float32)


def factor_pair(gram):
    size = gram.shape[0]
    if size == 1:
        root = jnp.sqrt(gram)
        return (root, 1.0 / root)
    half = size // 2
    first_up, first_inv = factor_pair(gram[:half, :half])
    coupling = cross_product(first_inv, gram[:half, half:])
    schur = gram[half:, half:] - cross_product(coupling, coupling)
    second_up, second_inv = factor_pair(schur)
    lower_zero = jnp.zeros((size - half, half), jnp.float32)
    upper = jnp.concatenate(
        [
            jnp.concatenate([first_up, coupling], axis=1),
            jnp.concatenate([lower_zero, second_up], axis=1),
        ],
        axis=0,
    )
    corner = -matmul(matmul(first_inv, coupling), second_inv)
    inverse = jnp.concatenate(
        [
            jnp.concatenate([first_inv, corner], axis=1),
            jnp.concatenate([lower_zero, second_inv], axis=1),
        ],
        axis=0,
    )
    return (upper, inverse)


def project_after(inverse, panel, local, summed):
    basis_rows = matmul(panel, inverse)
    top = summed(cross_product(basis_rows, local))
    residual = local - matmul(basis_rows, top)
    return (top, residual)


def per_device(matrix):
    rows_here = matrix.shape[0]
    blocks = matrix.shape[1]
    width = matrix.shape[3]
    local = matrix.reshape(rows_here, blocks * width)
    pieces = []
    for owner in range(2):
        pieces.append(broadcast(matrix[:, 0, 0, :], "col", owner))
    panel = jnp.concatenate(pieces, axis=1)
    total_rows = rows_here * lax.axis_size("row")
    gram = cross_product(panel, panel)
    upper, inverse = factor_pair(lax.psum(gram, "row"))

    def summed(value):
        return lax.psum(value, "row")

    top, residual = project_after(inverse, panel, local, summed)
    scaled = top / math.sqrt(total_rows)
    return (
        scaled.reshape(top.shape[0], blocks, 1, width),
        residual.reshape(rows_here, blocks, 1, width),
    )


def solution(mesh):
    return jax.shard_map(
        per_device,
        mesh=mesh,
        in_specs=(P("row", None, "col", None),),
        out_specs=(P(None, None, "col", None), P("row", None, "col", None)),
        check_vma=False,
    )
```

profile of v0, /device:TPU:1, one launch (start us, length us, event | category | flops | bytes accessed | tf_op | source)
XLA Modules:
  0.0 833.4 jit_solution(13384232351015259897)
XLA Ops:
  7.3 3.3 broadcast_select_fusion
  10.6 1.0 select_bitcast_fusion
  11.7 82.9 %all-reduce.136.cloned.1.call-done = (f32[2048,128]{1,0:T(8,128)}, f32[2048,128]{1,0:T(8,128)}) async-done(((f32[2048,128]{1,0:T(8,128)}, f32[2048,128]{1,0:T(8,128)}), (f32[2048,128]{1,0:T(8,128)}, f32[2048,128]{1,0:T(8,128)})) %all-reduce.136.cloned.1.call-update) | async-done | bytes 2097168 | tf_op jit(solution)/shard_map/psum | solution.py:10
  94.6 1.4 constant_dynamic-update-slice_fusion.1
  96.2 4.2 fusion.1342
  100.5 12.0 %copy.264 = f32[2048,5,1,128]{0,3,1,2:T(8,128)} copy(f32[2048,5,1,128]{3,2,1,0:T(1,128)} %param.1) | data formatting | bytes 10485760 | tf_op args[0]
  112.5 101.5 %all-reduce.132.cloned.1.call-done = f32[256,256]{1,0:T(8,128)} async-done(((f32[256,256]{1,0:T(8,128)}), f32[256,256]{1,0:T(8,128)}) %all-reduce.132.cloned.1.call-update) | async-done | bytes 262160 | tf_op jit(solution)/shard_map/psum | solution.py:74
  214.0 1.5 fusion.1214
  217.5 0.9 fusion.928
  218.6 0.9 convolution_subtract_fusion.127
  222.2 1.0 fusion.735
  223.4 0.9 convolution_subtract_fusion.63
  230.6 1.0 fusion.511
  231.8 0.9 convolution_subtract_fusion.31
  246.2 1.0 fusion.319
  247.4 0.9 convolution_subtract_fusion.15
  265.7 0.7 fusion.1335
  276.4 1.0 fusion.191
  277.6 0.9 convolution_subtract_fusion.7
  295.9 0.7 fusion.1331
  310.4 0.7 fusion.1329
  324.6 0.7 fusion.1327
  331.8 0.7 fusion.1326
  353.4 0.7 fusion.1323
  367.4 0.7 fusion.1321
  381.3 0.7 fusion.1319
  395.4 0.7 fusion.1317
  409.3 0.7 fusion.1315
  423.4 0.7 fusion.1313
  465.9 0.7 fusion.1307
  479.9 0.7 fusion.1305
  493.8 0.7 fusion.1303
  508.0 0.7 fusion.1301
  521.8 0.7 fusion.1299
  535.9 0.7 fusion.1297
  564.2 0.7 fusion.1293
  578.0 0.7 fusion.1291
  592.1 0.7 fusion.1289
  620.2 0.7 fusion.1285
  673.2 2.0 fusion
  675.2 1.3 copy-done
  676.4 13.2 %fusion.1408 = f32[256,640]{1,0:T(8,128)} fusion(f32[2048,256]{1,0:T(8,128)S(1)} %fusion, f32[2048,640]{0,1:T(8,128)} %bitcast.1420), kind=kOutput, calls=%fused_computation.1806 | convolution fusion | flops 4026531840 | bytes 7995392 | tf_op jit(solution)/shard_map/mk,mn->kn/dot_general | solution.py:14
  689.6 113.0 %all-reduce.134.cloned.1.call-done = f32[256,640]{1,0:T(8,128)} async-done(((f32[256,640]{1,0:T(8,128)}), f32[256,640]{1,0:T(8,128)}) %all-reduce.134.cloned.1.call-update) | async-done | bytes 655376 | tf_op jit(solution)/shard_map/psum | solution.py:77
  802.6 2.0 broadcast_multiply_fusion
  804.7 1.3 copy.265
  806.0 1.1 copy.266
  807.2 7.9 convolution_subtract_fusion
  815.1 11.5 %copy.267 = f32[2048,5,1,128]{3,2,1,0:T(1,128)} copy(f32[2048,5,1,128]{0,3,1,2:T(8,128)} %bitcast.1422) | data formatting | bytes 10485760
  (876 shorter events, 184.5 us)
Async XLA Ops:
  7.2 87.4 %all-reduce.136.cloned.1.call-start = ((), (), s32[]{:S(2)}) async-start(), calls=%async_computation.2 | async-start | bytes 4194304 | tf_op jit(solution)/shard_map/psum | solution.py:10
  11.6 202.3 %all-reduce.132.cloned.1.call-start = ((), (), s32[]{:S(2)}) async-start(), calls=%async_computation | async-start | bytes 524288 | tf_op jit(solution)/shard_map/psum | solution.py:74
  94.6 1.5 copy-start.3
  100.4 702.2 %all-reduce.134.cloned.1.call-start = ((), (), s32[]{:S(2)}) async-start(), calls=%async_computation.1 | async-start | bytes 1310720 | tf_op jit(solution)/shard_map/psum | solution.py:77
  214.0 121.7 %copy-start.4 = (f32[256,256]{1,0:T(8,128)S(1)}, f32[256,256]{1,0:T(8,128)}, u32[]{:S(2)}) copy-start(f32[256,256]{1,0:T(8,128)} %all-reduce.132.cloned.1.call-done) | copy-start | bytes 786436
  675.1 1.3 copy-start
  689.6 117.5 %copy-start.1 = (f32[2048,256]{1,0:T(8,128)S(1)}, f32[2048,256]{1,0:T(8,128)}, u32[]{:S(2)}) copy-start(f32[2048,256]{1,0:T(8,128)} %copy-done) | copy-start | bytes 6291460
  802.6 4.5 copy-start.2
Sparse Core Ops, SparseCore 0:
  11.8 82.7 all-reduce.135
  100.5 113.4 all-reduce.131
  689.7 112.8 all-reduce.133
where the time goes:
time: 842 us; the launch traced here: 833 us
  waiting for transfers between devices  297 us (35%)
  between operations  264 us (31%)
  matrix products  130 us (15%)
  local copies, waits for them, and re-layouts  120 us (14%)
  other arithmetic  22 us (3%)
    psum x1, waiting for transfers between devices, summed(): return lax.psum(value, 'row')  113 us
    psum x1, waiting for transfers between devices, per_device(): upper, inverse = factor_pair(lax.psum(gram, 'row'))  102 us
    slice x128, local copies, waits for them, and re-layouts, factor_pair(): coupling = cross_product(first_inv, gram[:half, half:])  86.2 us
    psum x1, waiting for transfers between devices, broadcast(): return lax.psum(jnp.where(mine, value, jnp.zeros_like(value)), axis)  82.9 us
    dot_general x256, matrix products, cross_product(): jnp.einsum('mk,mn->kn', left, right, precision=lax.Precision.HIGHEST, pre...  79.4 us
    dot_general x256, matrix products, matmul(): jnp.dot(left, right, precision=lax.Precision.HIGHEST, preferred_element_t...  50.2 us
    unnamed x14, local copies, waits for them, and re-layouts  27.5 us
  transfers between devices with their start and end apart: 3, of which 3 were waited for; matrix products, arithmetic and copies ran while one was open for 1% of the time, Pallas kernels for 0%

commit v1 on v0

--- a/solution.py
+++ b/solution.py
@@ -7,7 +7,7 @@
 
 def broadcast(value, axis, root):
     mine = lax.axis_index(axis) == root
-    return lax.psum(jnp.where(mine, value, jnp.zeros_like(value)), axis)
+    return jnp.sum(lax.all_gather(jnp.where(mine, value, jnp.zeros_like(value)), axis), axis=0)
 
 
 def cross_product(left, right):

time: 842 us -> 948 us (1.13)
  waiting for transfers between devices: 297 us -> 400 us
    all_gather x0 -> x2, waiting for transfers between devices: none -> 188 us  [broadcast(): lax.all_gather(jnp.where(mine, value, jnp.zeros_like(value)), axis)]
    psum x1 -> x0, waiting for transfers between devices: 82.9 us -> none  [broadcast(): return lax.psum(jnp.where(mine, value, jnp.zeros_like(value)), axis)]
    unnamed x14 -> x9, local copies, waits for them, and re-layouts: 27.5 us -> 24.7 us
  transfers between devices with their start and end apart: 3 -> 4, of which waited for: 3 -> 4; matrix products, arithmetic and copies ran while one was open for 1% -> 2% of each run, Pallas kernels for 0% -> 0%
where the time goes in v1:
time: 948 us; the launch traced here: 939 us
  waiting for transfers between devices  400 us (42%)
  between operations  263 us (28%)
  matrix products  130 us (14%)
  local copies, waits for them, and re-layouts  117 us (12%)
  other arithmetic  29 us (3%)
    all_gather x2, waiting for transfers between devices, broadcast(): lax.all_gather(jnp.where(mine, value, jnp.zeros_like(value)), axis)  188 us
    psum x1, waiting for transfers between devices, summed(): return lax.psum(value, 'row')  113 us
    psum x1, waiting for transfers between devices, per_device(): upper, inverse = factor_pair(lax.psum(gram, 'row'))  98 us
    slice x128, local copies, waits for them, and re-layouts, factor_pair(): coupling = cross_product(first_inv, gram[:half, half:])  86 us
    dot_general x256, matrix products, cross_product(): jnp.einsum('mk,mn->kn', left, right, precision=lax.Precision.HIGHEST, pre...  78.9 us
    dot_general x256, matrix products, matmul(): jnp.dot(left, right, precision=lax.Precision.HIGHEST, preferred_element_t...  51.4 us
    unnamed x9, local copies, waits for them, and re-layouts  24.7 us
  transfers between devices with their start and end apart: 4, of which 4 were waited for; matrix products, arithmetic and copies ran while one was open for 2% of the time, Pallas kernels for 0%

profile of v1, /device:TPU:1, one launch (start us, length us, event | category | flops | bytes accessed | tf_op | source)
XLA Modules:
  0.0 939.2 jit_solution(10216093612583078460)
XLA Ops:
  7.2 3.5 broadcast_select_fusion.1
  10.8 0.7 all-gather.7.cloned.1.call-update
  11.5 97.3 %all-gather.5.cloned.1.call-done = f32[16384,1,1,128]{3,2,1,0:T(1,128)} async-done(((f32[2048,1,1,128]{3,2,1,0:T(1,128)}), f32[16384,1,1,128]{3,2,1,0:T(1,128)}) %all-gather.5.cloned.1.call-update) | async-done | bytes 8388624 | tf_op jit(solution)/shard_map/all_gather | solution.py:10
  108.8 3.9 reduce_sum.18
  112.7 90.7 %all-gather.7.cloned.1.call-done = f32[16384,1,1,128]{3,2,1,0:T(1,128)} async-done(((f32[2048,1,1,128]{3,2,1,0:T(1,128)}), f32[16384,1,1,128]{3,2,1,0:T(1,128)}) %all-gather.7.cloned.1.call-update) | async-done | bytes 8388624 | tf_op jit(solution)/shard_map/all_gather | solution.py:10
  203.4 3.9 reduce_sum.19
  207.3 4.2 fusion.1
  211.6 12.0 %copy.392 = f32[2048,5,1,128]{0,3,1,2:T(8,128)} copy(f32[2048,5,1,128]{3,2,1,0:T(1,128)} %param.1) | data formatting | bytes 10485760 | tf_op args[0]
  223.6 98.0 %all-reduce.130.cloned.1.call-done = f32[256,256]{1,0:T(8,128)} async-done(((f32[256,256]{1,0:T(8,128)}), f32[256,256]{1,0:T(8,128)}) %all-reduce.130.cloned.1.call-update) | async-done | bytes 262160 | tf_op jit(solution)/shard_map/psum | solution.py:74
  321.6 1.5 fusion.1216
  325.1 0.8 fusion.928
  326.1 0.9 convolution_subtract_fusion.127
  329.6 0.9 fusion.736
  330.8 0.9 convolution_subtract_fusion.63
  337.7 0.9 fusion.512
  338.9 0.9 convolution_subtract_fusion.31
  349.6 0.7 fusion.1340
  352.9 1.0 fusion.320
  354.1 0.9 convolution_subtract_fusion.15
  364.8 0.7 fusion.1338
  371.8 0.7 fusion.1337
  382.3 1.0 fusion.192
  383.5 0.9 convolution_subtract_fusion.7
  401.3 0.7 fusion.1333
  415.4 0.7 fusion.1331
  429.3 0.7 fusion.1329
  486.0 0.7 fusion.1321
  514.3 0.7 fusion.1317
  528.5 0.7 fusion.1315
  542.5 0.7 fusion.1313
  599.3 0.7 fusion.1305
  627.7 0.7 fusion.1301
  641.8 0.7 fusion.1299
  655.8 0.7 fusion.1297
  684.3 0.7 fusion.1293
  698.5 0.7 fusion.1291
  712.5 0.7 fusion.1289
  726.8 0.7 fusion.1287
  740.7 0.7 fusion.1285
  754.8 0.7 fusion.1283
  779.5 3.1 fusion
  782.7 12.8 %fusion.1409 = f32[256,640]{1,0:T(8,128)} fusion(f32[2048,256]{1,0:T(8,128)S(1)} %fusion, f32[2048,640]{0,1:T(8,128)} %bitcast.1414), kind=kOutput, calls=%fused_computation.1806 | convolution fusion | flops 4026531840 | bytes 7995392 | tf_op jit(solution)/shard_map/mk,mn->kn/dot_general | solution.py:14
  795.5 113.0 %all-reduce.132.cloned.1.call-done = f32[256,640]{1,0:T(8,128)} async-done(((f32[256,640]{1,0:T(8,128)}), f32[256,640]{1,0:T(8,128)}) %all-reduce.132.cloned.1.call-update) | async-done | bytes 655376 | tf_op jit(solution)/shard_map/psum | solution.py:77
  908.5 2.0 broadcast_multiply_fusion
  910.5 1.3 copy.393
  911.8 1.1 copy.394
  913.0 7.9 convolution_subtract_fusion
  920.9 11.5 %copy.395 = f32[2048,5,1,128]{3,2,1,0:T(1,128)} copy(f32[2048,5,1,128]{0,3,1,2:T(8,128)} %bitcast.1416) | data formatting | bytes 10485760
  (873 shorter events, 184.7 us)
Async XLA Ops:
  7.2 101.7 %all-gather.5.cloned.1.call-start = ((), (), s32[]{:S(2)}) async-start(), calls=%async_computation.2 | async-start | bytes 9437184 | tf_op jit(solution)/shard_map/all_gather | solution.py:10
  10.7 192.7 %all-gather.7.cloned.1.call-start = ((), (), s32[]{:S(2)}) async-start(), calls=%async_computation.3 | async-start | bytes 9437184 | tf_op jit(solution)/shard_map/all_gather | solution.py:10
  11.5 310.1 %all-reduce.130.cloned.1.call-start = ((), (), s32[]{:S(2)}) async-start(), calls=%async_computation | async-start | bytes 524288 | tf_op jit(solution)/shard_map/psum | solution.py:74
  207.3 16.3 %copy-start = (f32[2048,128]{1,0:T(8,128)}, f32[2048,128]{1,0:T(8,128)S(1)}, u32[]{:S(2)}) copy-start(f32[2048,128]{1,0:T(8,128)S(1)} %reduce_sum.19) | copy-start | bytes 3145732
  211.5 697.0 %all-reduce.132.cloned.1.call-start = ((), (), s32[]{:S(2)}) async-start(), calls=%async_computation.1 | async-start | bytes 1310720 | tf_op jit(solution)/shard_map/psum | solution.py:77
  321.6 118.6 %copy-start.2 = (f32[256,256]{1,0:T(8,128)S(1)}, f32[256,256]{1,0:T(8,128)}, u32[]{:S(2)}) copy-start(f32[256,256]{1,0:T(8,128)} %all-reduce.130.cloned.1.call-done) | copy-start | bytes 786436
  908.5 4.5 copy-start.1
Sparse Core Ops, SparseCore 0:
  10.9 97.9 all-gather.4
  110.6 92.7 all-gather.6
  211.6 109.8 all-reduce.129
  795.6 112.8 all-reduce.131
